TPU v7x, 32 devices: a whole 2x2x4 slice. The times are simulated.
32 devices in a mesh: fsdp: 8 (over z, y), ctx: 2 (over x), tp: 2 (over core).
Axes of the slice: x: 2, y: 2, z: 4, core: 2. Of those that a mesh axis runs over, the one named last changes fastest.
Arguments:
- tokens_in: bfloat16 [4096, 2048], P(('fsdp', 'ctx')), may hold values from -6 to 6
- doc_positions: int32 [4096], P(('fsdp', 'ctx')), may hold values from 0 to 383, as said below
- attn_gain: bfloat16 [2048], P('fsdp'), may hold values from 0.25 to 1.75
- query_weight: bfloat16 [2048, 2048], P('fsdp', 'tp'), may hold values from -1 to 1
- key_weight: bfloat16 [2048, 256], P('fsdp', 'tp'), may hold values from -1 to 1
- value_weight: bfloat16 [2048, 256], P('fsdp', 'tp'), may hold values from -0.125 to 0.125
- output_weight: bfloat16 [2048, 2048], P('fsdp', 'tp'), may hold values from -2 to 2
- mlp_gain: bfloat16 [2048], P('fsdp'), may hold values from 0.25 to 1.75
- gate_weight: bfloat16 [2048, 5632], P('fsdp', 'tp'), may hold values from -0.125 to 0.125
- up_weight: bfloat16 [2048, 5632], P('fsdp', 'tp'), may hold values from -0.125 to 0.125
- down_weight: bfloat16 [2048, 5632], P('fsdp', 'tp'), may hold values from -0.078125 to 0.078125
- cotangent: bfloat16 [4096, 2048], P(('fsdp', 'ctx')), may hold values from -6 to 6
Outputs:
- block_out: bfloat16 [4096, 2048], P(('fsdp', 'ctx'))
- grad_tokens: float32 [4096, 2048], P(('fsdp', 'ctx'))
- grad_attn_gain: float32 [2048], P('fsdp')
- grad_query: float32 [2048, 2048], P('fsdp', 'tp')
- grad_key: float32 [2048, 256], P('fsdp', 'tp')
- grad_value: float32 [2048, 256], P('fsdp', 'tp')
- grad_output: float32 [2048, 2048], P('fsdp', 'tp')
- grad_mlp_gain: float32 [2048], P('fsdp')
- grad_gate: float32 [2048, 5632], P('fsdp', 'tp')
- grad_up: float32 [2048, 5632], P('fsdp', 'tp')
- grad_down: float32 [2048, 5632], P('fsdp', 'tp')
Inputs may be any that keep to these rules, and one draw needn't show every extreme that they name: `doc_positions`: each sequence of 512 tokens is packed with documents and begins with a new one; a token's value is its offset within its document: 0 at a document's first token, rising by one along it. Documents hold 102 to 384 tokens, except that the last of a sequence may be cut short; some document holds exactly 384.
All inputs are finite; a program needn't handle non-finite values.
Results may differ from a plain program's by a relative error of at most 0.014.
The roundings to bfloat16 on the way count: a program that leaves them out, or rounds other values in their place, can miss the bound.
Values may be sent and summed in bfloat16 or wider, within the bound.
No kernel may reach another device: no remote copies, remote signals or barrier semaphores. Data moves between devices by JAX's collectives and lax.ppermute only.
A program may use at most 256 MiB of HBM per device.

v0:
```python
import jax
import jax.numpy as jnp
from jax import lax
from jax.sharding import PartitionSpec as P

HEADS = 32
KV_HEADS = 4
HEAD_DIM = 64
EPSILON = 1e-05
NEG_FILL = -1e30


def rotary_tables(positions):
    half_dim = HEAD_DIM // 2
    inverse = 1.0 / 10000.0 ** (jnp.arange(half_dim, dtype=jnp.float32) * (2.0 / HEAD_DIM))
    angles = positions.astype(jnp.float32)[:, None] * inverse[None, :]
    cosine_table = jnp.concatenate([jnp.cos(angles), jnp.cos(angles)], axis=-1)[:, None, :]
    sine_table = jnp.concatenate([jnp.sin(angles), jnp.sin(angles)], axis=-1)[:, None, :]
    return (cosine_table, sine_table)


def apply_rotary(values, cosine_table, sine_table):
    half_dim = values.shape[-1] // 2
    turned = jnp.concatenate([-values[..., half_dim:], values[..., :half_dim]], axis=-1)
    return values * cosine_table + turned * sine_table


def undo_rotary(gradient, cosine_table, sine_table):
    half_dim = gradient.shape[-1] // 2
    sined = gradient * sine_table
    return gradient * cosine_table + jnp.concatenate(
        [sined[..., half_dim:], -sined[..., :half_dim]], axis=-1
    )


def contract_last(left_array, right_array):
    return lax.dot_general(
        left_array, right_array, (((1,), (1,)), ((), ())), preferred_element_type=jnp.float32
    )


def contract_first(left_array, right_array):
    return lax.dot_general(
        left_array, right_array, (((0,), (0,)), ((), ())), preferred_element_type=jnp.float32
    )


def normed_fold(scaled, pieces):
    gain_float = pieces[0].astype(jnp.float32)
    normed = (scaled * gain_float[None, :]).astype(jnp.bfloat16)
    sums = tuple(
        (jnp.dot(normed, matrix, preferred_element_type=jnp.float32) for matrix in pieces[1:])
    )
    return sums + (normed, gain_float)


def row_fold(left_array, shard_piece):
    return jnp.dot(left_array, shard_piece, preferred_element_type=jnp.float32)


def column_fold(gradients_in, pieces):
    part_sum = contract_last(gradients_in[0], pieces[0])
    for grad_piece, weight_piece in zip(gradients_in[1:], pieces[1:]):
        part_sum = part_sum + contract_last(grad_piece, weight_piece)
    return part_sum


def column_map(left_array, shard_piece):
    return contract_last(left_array, shard_piece)


def tensor_total(partial_sum):
    return lax.psum(partial_sum, "tp")


def body(
    tokens_in,
    doc_positions,
    attn_gain,
    query_weight,
    key_weight,
    value_weight,
    output_weight,
    mlp_gain,
    gate_weight,
    up_weight,
    down_weight,
    cotangent,
):
    local_rows = tokens_in.shape[0]
    query_columns = query_weight.shape[1]
    key_columns = key_weight.shape[1]
    local_groups = key_columns // HEAD_DIM
    group_size = HEADS // KV_HEADS
    group_width = group_size * HEAD_DIM
    score_scale = HEAD_DIM ** (-0.5)
    tokens = tokens_in.astype(jnp.float32)
    rms_one = lax.rsqrt(jnp.mean(tokens * tokens, axis=-1, keepdims=True) + EPSILON)
    scaled_one = tokens * rms_one
    query_lin, key_lin, value_lin, normed_one, gain_one = normed_fold(
        scaled_one,
        (
            lax.all_gather(attn_gain, "fsdp", axis=0, tiled=True),
            lax.all_gather(query_weight, "fsdp", axis=0, tiled=True),
            lax.all_gather(key_weight, "fsdp", axis=0, tiled=True),
            lax.all_gather(value_weight, "fsdp", axis=0, tiled=True),
        ),
    )
    cosine_table, sine_table = rotary_tables(doc_positions)
    queries = (
        apply_rotary(query_lin.reshape(local_rows, -1, HEAD_DIM), cosine_table, sine_table)
        .astype(jnp.bfloat16)
        .reshape(local_rows, query_columns)
    )
    keys_low = (
        apply_rotary(key_lin.reshape(local_rows, -1, HEAD_DIM), cosine_table, sine_table)
        .astype(jnp.bfloat16)
        .reshape(local_rows, key_columns)
    )
    values_low = value_lin.astype(jnp.bfloat16)
    key_all, value_all = (
        lax.all_gather(keys_low, "ctx", axis=0, tiled=True),
        lax.all_gather(values_low, "ctx", axis=0, tiled=True),
    )
    key_count = key_all.shape[0]
    query_places = lax.axis_index("ctx") * local_rows + jnp.arange(local_rows, dtype=jnp.int32)
    key_places = jnp.arange(key_count, dtype=jnp.int32)
    allowed = (key_places[None, :] <= query_places[:, None]) & (
        key_places[None, :] >= (query_places - doc_positions)[:, None]
    )

    def head_scores(query_group, key_head):
        raw_scores = (
            jnp.einsum("ngd,kd->gnk", query_group, key_head, preferred_element_type=jnp.float32)
            * score_scale
        )
        return jnp.where(allowed[None], raw_scores, NEG_FILL)

    attended_parts = []
    lse_parts = []
    for group_index in range(local_groups):
        query_group = queries[
            :, group_index * group_width : (group_index + 1) * group_width
        ].reshape(local_rows, group_size, HEAD_DIM)
        key_head = key_all[:, group_index * HEAD_DIM : (group_index + 1) * HEAD_DIM]
        value_head = value_all[:, group_index * HEAD_DIM : (group_index + 1) * HEAD_DIM]
        scores = head_scores(query_group, key_head)
        largest = jnp.max(scores, axis=-1, keepdims=True)
        exponent = jnp.exp(scores - largest)
        totals = jnp.sum(exponent, axis=-1, keepdims=True)
        probs_low = (exponent / totals).astype(jnp.bfloat16)
        attended_parts.append(
            jnp.einsum(
                "gnk,kd->ngd", probs_low, value_head, preferred_element_type=jnp.float32
            ).reshape(local_rows, group_width)
        )
        lse_parts.append(largest + jnp.log(totals))
    attended_low = jnp.concatenate(attended_parts, axis=1).astype(jnp.bfloat16)
    attn_branch = tensor_total(
        column_map(attended_low, lax.all_gather(output_weight, "fsdp", axis=0, tiled=True))
    )
    residual = tokens + attn_branch
    rms_two = lax.rsqrt(jnp.mean(residual * residual, axis=-1, keepdims=True) + EPSILON)
    scaled_two = residual * rms_two
    gate_lin, up_lin, normed_two, gain_two = normed_fold(
        scaled_two,
        (
            lax.all_gather(mlp_gain, "fsdp", axis=0, tiled=True),
            lax.all_gather(gate_weight, "fsdp", axis=0, tiled=True),
            lax.all_gather(up_weight, "fsdp", axis=0, tiled=True),
        ),
    )
    silu_value = gate_lin / (1.0 + jnp.exp(-gate_lin))
    act_low = (silu_value * up_lin).astype(jnp.bfloat16)
    mlp_branch = tensor_total(
        column_map(act_low, lax.all_gather(down_weight, "fsdp", axis=0, tiled=True))
    )
    block_out = (residual + mlp_branch).astype(jnp.bfloat16)
    grad_out = cotangent.astype(jnp.float32)
    grad_act = row_fold(cotangent, lax.all_gather(down_weight, "fsdp", axis=0, tiled=True))
    sigmoid = 1.0 / (1.0 + jnp.exp(-gate_lin))
    grad_gate_lin = (grad_act * up_lin * sigmoid * (1.0 + gate_lin * (1.0 - sigmoid))).astype(
        jnp.bfloat16
    )
    grad_up_lin = (grad_act * silu_value).astype(jnp.bfloat16)
    grad_normed_two = tensor_total(
        column_fold(
            (grad_gate_lin, grad_up_lin),
            (
                lax.all_gather(gate_weight, "fsdp", axis=0, tiled=True),
                lax.all_gather(up_weight, "fsdp", axis=0, tiled=True),
            ),
        )
    )
    scaled_grad_two = grad_normed_two * gain_two[None, :]
    grad_residual = (
        grad_out
        + rms_two * scaled_grad_two
        - residual
        * (rms_two * rms_two * rms_two)
        * jnp.mean(scaled_grad_two * residual, axis=-1, keepdims=True)
    )
    grad_attn_low = grad_residual.astype(jnp.bfloat16)
    grad_attended = row_fold(
        grad_attn_low, lax.all_gather(output_weight, "fsdp", axis=0, tiled=True)
    ).astype(jnp.bfloat16)
    query_grads = []
    key_grads = []
    value_grads = []
    for group_index in range(local_groups):
        query_group = queries[
            :, group_index * group_width : (group_index + 1) * group_width
        ].reshape(local_rows, group_size, HEAD_DIM)
        key_head = key_all[:, group_index * HEAD_DIM : (group_index + 1) * HEAD_DIM]
        value_head = value_all[:, group_index * HEAD_DIM : (group_index + 1) * HEAD_DIM]
        probabilities = jnp.exp(head_scores(query_group, key_head) - lse_parts[group_index])
        probs_low = probabilities.astype(jnp.bfloat16)
        grad_group = grad_attended[
            :, group_index * group_width : (group_index + 1) * group_width
        ].reshape(local_rows, group_size, HEAD_DIM)
        grad_probs = jnp.einsum(
            "ngd,kd->gnk", grad_group, value_head, preferred_element_type=jnp.float32
        )
        row_dot = jnp.sum(probabilities * grad_probs, axis=-1, keepdims=True)
        grad_scores = (probabilities * (grad_probs - row_dot)).astype(jnp.bfloat16)
        query_grads.append(
            jnp.einsum("gnk,kd->ngd", grad_scores, key_head, preferred_element_type=jnp.float32)
            * score_scale
        )
        key_grads.append(
            jnp.einsum("gnk,ngd->kd", grad_scores, query_group, preferred_element_type=jnp.float32)
            * score_scale
        )
        value_grads.append(
            jnp.einsum("gnk,ngd->kd", probs_low, grad_group, preferred_element_type=jnp.float32)
        )
    key_grad_local, value_grad_local = (
        lax.psum_scatter(
            jnp.concatenate(key_grads, axis=1), "ctx", scatter_dimension=0, tiled=True
        ),
        lax.psum_scatter(
            jnp.concatenate(value_grads, axis=1), "ctx", scatter_dimension=0, tiled=True
        ),
    )
    grad_q_lin = (
        undo_rotary(jnp.concatenate(query_grads, axis=1), cosine_table, sine_table)
        .astype(jnp.bfloat16)
        .reshape(local_rows, query_columns)
    )
    grad_k_lin = (
        undo_rotary(key_grad_local.reshape(local_rows, -1, HEAD_DIM), cosine_table, sine_table)
        .astype(jnp.bfloat16)
        .reshape(local_rows, key_columns)
    )
    grad_v_lin = value_grad_local.astype(jnp.bfloat16)
    grad_normed_one = tensor_total(
        column_fold(
            (grad_q_lin, grad_k_lin, grad_v_lin),
            (
                lax.all_gather(query_weight, "fsdp", axis=0, tiled=True),
                lax.all_gather(key_weight, "fsdp", axis=0, tiled=True),
                lax.all_gather(value_weight, "fsdp", axis=0, tiled=True),
            ),
        )
    )
    scaled_grad_one = grad_normed_one * gain_one[None, :]
    grad_tokens = (
        grad_residual
        + rms_one * scaled_grad_one
        - tokens
        * (rms_one * rms_one * rms_one)
        * jnp.mean(scaled_grad_one * tokens, axis=-1, keepdims=True)
    )
    owned = lax.psum_scatter(
        (
            jnp.sum(grad_normed_one * scaled_one, axis=0),
            contract_first(normed_one, grad_q_lin),
            contract_first(normed_one, grad_k_lin),
            contract_first(normed_one, grad_v_lin),
            contract_first(grad_attn_low, attended_low),
            jnp.sum(grad_normed_two * scaled_two, axis=0),
            contract_first(normed_two, grad_gate_lin),
            contract_first(normed_two, grad_up_lin),
            contract_first(cotangent, act_low),
        ),
        "fsdp",
        scatter_dimension=0,
        tiled=True,
    )
    (
        gain_one_grad,
        query_grad,
        key_grad,
        value_grad,
        output_grad,
        gain_two_grad,
        gate_grad,
        up_grad,
        down_grad,
    ) = owned
    summed = lax.psum(
        (
            gain_one_grad,
            query_grad,
            key_grad,
            value_grad,
            output_grad,
            gain_two_grad,
            gate_grad,
            up_grad,
            down_grad,
        ),
        "ctx",
    )
    return (
        block_out,
        grad_tokens,
        summed[0],
        summed[1],
        summed[2],
        summed[3],
        summed[4],
        summed[5],
        summed[6],
        summed[7],
        summed[8],
    )


def solution(mesh):
    return jax.shard_map(
        body,
        mesh=mesh,
        in_specs=(
            P(("fsdp", "ctx"), None),
            P(("fsdp", "ctx")),
            P("fsdp"),
            P("fsdp", "tp"),
            P("fsdp", "tp"),
            P("fsdp", "tp"),
            P("fsdp", "tp"),
            P("fsdp"),
            P("fsdp", "tp"),
            P("fsdp", "tp"),
            P("fsdp", "tp"),
            P(("fsdp", "ctx"), None),
        ),
        out_specs=(
            P(("fsdp", "ctx"), None),
            P(("fsdp", "ctx"), None),
            P("fsdp"),
            P("fsdp", "tp"),
            P("fsdp", "tp"),
            P("fsdp", "tp"),
            P("fsdp", "tp"),
            P("fsdp"),
            P("fsdp", "tp"),
            P("fsdp", "tp"),
            P("fsdp", "tp"),
        ),
        check_vma=False,
    )
```

profile of v0, /device:TPU:0, one launch (start us, length us, event | category | flops | bytes accessed | tf_op | source)
XLA Modules:
  0.0 2660.1 jit_solution(7111655742602666391)
XLA Ops:
  9.4 22.6 all-gather
  35.1 33.7 %all_gather.43 = bf16[2048,128]{1,0:T(8,128)(2,1)S(1)} all-gather(bf16[256,128]{1,0:T(8,128)(2,1)S(1)} %copy-done.46), channel_id=1, replica_groups=mesh['fsdp'=8,'ctx'=2,'tp'=2] {'fsdp'}, dimensions={0}, use_global_device_ids=true | all-gather | bytes 589824 | tf_op jit(solution)/shard_map/all_gather | solution.py:105
  70.0 5.0 all_gather.44
  75.1 32.7 %all_gather.41 = bf16[2048,128]{1,0:T(8,128)(2,1)S(1)} all-gather(bf16[256,128]{1,0:T(8,128)(2,1)S(1)} %copy-done.47), channel_id=1, replica_groups=mesh['fsdp'=8,'ctx'=2,'tp'=2] {'fsdp'}, dimensions={0}, use_global_device_ids=true | all-gather | bytes 589824 | tf_op jit(solution)/shard_map/all_gather | solution.py:106
  108.3 5.0 all_gather.42
  114.1 3.5 fusion.62
  121.3 2.5 copy.72
  131.4 39.2 %all-gather.10.cloned.1.call-done = bf16[2048,1024]{1,0:T(8,128)(2,1)} async-done(((bf16[256,1024]{1,0:T(8,128)(2,1)}), bf16[2048,1024]{1,0:T(8,128)(2,1)}) %all-gather.10.cloned.1.call-update) | async-done | bytes 4194320 | tf_op jit(solution)/shard_map/all_gather | solution.py:160
  170.7 4.8 fusion.44
  177.3 18.3 all-gather.1
  200.0 162.1 %all-gather.14.cloned.1.call-done = bf16[2048,2816]{1,0:T(8,128)(2,1)} async-done(((bf16[256,2816]{1,0:T(8,128)(2,1)}), bf16[2048,2816]{1,0:T(8,128)(2,1)}) %all-gather.14.cloned.1.call-update) | async-done | bytes 11534352 | tf_op jit(solution)/shard_map/all_gather | solution.py:170
  362.1 9.3 fusion.74
  371.4 154.2 %all-gather.12.cloned.1.call-done = bf16[2048,2816]{1,0:T(8,128)(2,1)} async-done(((bf16[256,2816]{1,0:T(8,128)(2,1)}), bf16[2048,2816]{1,0:T(8,128)(2,1)}) %all-gather.12.cloned.1.call-update) | async-done | bytes 11534352 | tf_op jit(solution)/shard_map/all_gather | solution.py:169
  525.6 9.3 fusion.73
  534.9 154.2 %all-gather.16.cloned.1.call-done = bf16[2048,2816]{1,0:T(8,128)(2,1)} async-done(((bf16[256,2816]{1,0:T(8,128)(2,1)}), bf16[2048,2816]{1,0:T(8,128)(2,1)}) %all-gather.16.cloned.1.call-update) | async-done | bytes 11534352 | tf_op jit(solution)/shard_map/all_gather | solution.py:176
  689.2 11.1 multiply_convert_fusion
  700.3 7.1 fusion.76
  707.4 8.8 convolution_add_fusion.2
  718.9 16.9 all-reduce.13.cloned.1.call-done
  735.8 2.9 multiply_reduce_fusion
  744.9 3.8 fusion.34
  748.7 3.5 fusion
  754.0 3.1 fusion.31
  757.6 3.5 fusion.3
  761.9 4.4 fusion.2
  771.9 3.0 reduce-scatter.12.cloned.1.call-done
  774.9 2.5 fusion.51
  777.8 11.7 reduce-scatter.10.cloned.1.call-done
  793.0 6.3 fusion.40
  800.2 2.2 fusion.27
  804.3 4.8 fusion.60
  809.2 12.6 convolution_bitcast_fusion
  821.8 12.6 fusion.79
  834.7 12.6 fusion.78
  847.5 9.4 fusion.75
  861.1 63.5 %reduce-scatter.16.cloned.1.call-done = f32[256,128]{1,0:T(8,128)} async-done(((f32[2048,128]{1,0:T(8,128)}), f32[256,128]{1,0:T(8,128)}) %reduce-scatter.16.cloned.1.call-update) | async-done | bytes 131088 | tf_op jit(solution)/shard_map/reduce_scatter | solution.py:274
  924.6 149.9 %reduce-scatter.20.cloned.1.call-done = f32[256,1024]{1,0:T(8,128)} async-done(((f32[2048,1024]{1,0:T(8,128)}), f32[256,1024]{1,0:T(8,128)}) %reduce-scatter.20.cloned.1.call-update) | async-done | bytes 1048592 | tf_op jit(solution)/shard_map/reduce_scatter | solution.py:274
  1074.5 150.2 %reduce-scatter.14.cloned.1.call-done = f32[256,1024]{1,0:T(8,128)} async-done(((f32[2048,1024]{1,0:T(8,128)}), f32[256,1024]{1,0:T(8,128)}) %reduce-scatter.14.cloned.1.call-update) | async-done | bytes 1048592 | tf_op jit(solution)/shard_map/reduce_scatter | solution.py:274
  1224.8 376.5 %reduce-scatter.26.cloned.1.call-done = f32[256,2816]{0,1:T(8,128)} async-done(((f32[2048,2816]{0,1:T(8,128)}), f32[256,2816]{0,1:T(8,128)}) %reduce-scatter.26.cloned.1.call-update) | async-done | bytes 2883600 | tf_op jit(solution)/shard_map/reduce_scatter | solution.py:274
  1601.3 375.6 %reduce-scatter.24.cloned.1.call-done = f32[256,2816]{1,0:T(8,128)} async-done(((f32[2048,2816]{1,0:T(8,128)}), f32[256,2816]{1,0:T(8,128)}) %reduce-scatter.24.cloned.1.call-update) | async-done | bytes 2883600 | tf_op jit(solution)/shard_map/reduce_scatter | solution.py:274
  1976.9 375.6 %reduce-scatter.22.cloned.1.call-done = f32[256,2816]{1,0:T(8,128)} async-done(((f32[2048,2816]{1,0:T(8,128)}), f32[256,2816]{1,0:T(8,128)}) %reduce-scatter.22.cloned.1.call-update) | async-done | bytes 2883600 | tf_op jit(solution)/shard_map/reduce_scatter | solution.py:274
  2354.5 28.6 %all-reduce.15.cloned.1.call-done = (f32[256,2048]{1,0:T(8,128)}, f32[256,2048]{1,0:T(8,128)}) async-done(((f32[256,2048]{1,0:T(8,128)}, f32[256,2048]{1,0:T(8,128)}), (f32[256,2048]{1,0:T(8,128)}, f32[256,2048]{1,0:T(8,128)})) %all-reduce.15.cloned.1.call-update) | async-done | bytes 4194320 | tf_op jit(solution)/shard_map/psum | solution.py:73
  2383.1 2.3 fusion.14
  2385.3 37.3 %all-reduce.2 = (f32[2048]{0:T(1024)S(1)}, f32[2048]{0:T(1024)S(1)}) all-reduce(f32[2048]{0:T(1024)S(1)} %get-tuple-element.46, f32[2048]{0:T(1024)S(1)} %copy-done.52), channel_id=4, replica_groups=mesh['fsdp'=8,'ctx'=2,'tp'=2] {'fsdp'}, use_global_device_ids=true, to_apply=%region_17.18.clone | all-reduce | flops 4096 | bytes 32768
  2422.8 5.7 all-reduce.4
  2428.5 5.1 fusion.21
  2433.6 208.2 %all-reduce.17.cloned.1.call-done = (f32[256,1024]{1,0:T(8,128)}, f32[256,128]{1,0:T(8,128)}, f32[256,128]{1,0:T(8,128)}, f32[256,1024]{1,0:T(8,128)}, f32[256,2...) async-done(((f32[256,1024]{1,0:T(8,128)}, f32[256,128]{1,0:T(8,128)}, f32[256,128]{1,0:T(8,128)}, f32[256,1024]{1,0:T(8,128)}, f32[256,2816]{1,0:T(8,128)}, ...) | async-done | bytes 11010064 | tf_op jit(solution)/shard_map/psum | solution.py:301
  2641.9 3.5 copy.89
  (235 shorter events, 62.6 us)
Async XLA Ops:
  7.2 61.7 %copy-start.5 = (bf16[256,2048]{1,0:T(8,128)(2,1)S(1)}, bf16[256,2048]{1,0:T(8,128)(2,1)}, u32[]{:S(2)}) copy-start(bf16[256,2048]{1,0:T(8,128)(2,1)} %param.12) | copy-start | bytes 3145732
  7.2 28.0 %copy-start.46 = (bf16[256,128]{1,0:T(8,128)(2,1)S(1)}, bf16[256,128]{1,0:T(8,128)(2,1)}, u32[]{:S(2)}) copy-start(bf16[256,128]{1,0:T(8,128)(2,1)} %param.16) | copy-start | bytes 196612
  7.2 106.9 %all-gather.8.cloned.1.call-start = ((), (), s32[]{:S(2)}) async-start(), calls=%async_computation.9 | async-start | bytes 4718592 | tf_op jit(solution)/shard_map/all_gather | solution.py:104
  7.9 162.7 %all-gather.10.cloned.1.call-start = ((), (), s32[]{:S(2)}) async-start(), calls=%async_computation.10 | async-start | bytes 4718592 | tf_op jit(solution)/shard_map/all_gather | solution.py:160
  8.7 187.0 %all-reduce.11.cloned.1.call-start = ((), (), s32[]{:S(2)}) async-start(), calls=%async_computation.11 | async-start | bytes 4194304 | tf_op jit(solution)/shard_map/psum | solution.py:73
  35.1 79.0 %copy-start.48 = (f32[256]{0:T(256)}, f32[256]{0:T(256)S(1)}, u32[]{:S(2)}) copy-start(f32[256]{0:T(256)S(1)} %get-tuple-element.83) | copy-start | bytes 3076
  69.5 5.6 copy-start.47
  107.8 6.3 copy-start.21
  130.6 40.1 %copy-start.37 = (bf16[64,8,256]{2,0,1:T(8,128)(2,1)}, bf16[64,8,256]{2,0,1:T(8,128)(2,1)S(1)}, u32[]{:S(2)}) copy-start(bf16[64,8,256]{2,0,1:T(8,128)(2,1)S(1)} %fusion.29) | copy-start | bytes 786436
  131.4 44.1 %copy-start.38 = (bf16[64,8,256]{2,0,1:T(8,128)(2,1)}, bf16[64,8,256]{2,0,1:T(8,128)(2,1)S(1)}, u32[]{:S(2)}) copy-start(bf16[64,8,256]{2,0,1:T(8,128)(2,1)S(1)} %fusion.30) | copy-start | bytes 786436
  175.5 186.5 %all-gather.14.cloned.1.call-start = ((), (), s32[]{:S(2)}) async-start(), calls=%async_computation.13 | async-start | bytes 12976128 | tf_op jit(solution)/shard_map/all_gather | solution.py:170
  176.1 349.5 %all-gather.12.cloned.1.call-start = ((), (), s32[]{:S(2)}) async-start(), calls=%async_computation.12 | async-start | bytes 12976128 | tf_op jit(solution)/shard_map/all_gather | solution.py:169
  176.7 512.5 %all-gather.16.cloned.1.call-start = ((), (), s32[]{:S(2)}) async-start(), calls=%async_computation.14 | async-start | bytes 12976128 | tf_op jit(solution)/shard_map/all_gather | solution.py:176
  177.3 558.6 %all-reduce.13.cloned.1.call-start = ((), (), s32[]{:S(2)}) async-start(), calls=%async_computation.15 | async-start | bytes 4194304 | tf_op jit(solution)/shard_map/psum | solution.py:73
  700.3 7.1 copy-start.25
  700.3 7.1 copy-start.26
  716.2 58.7 %reduce-scatter.12.cloned.1.call-start = ((), (), s32[]{:S(2)}) async-start(), calls=%async_computation.17 | async-start | bytes 393216 | tf_op jit(solution)/shard_map/reduce_scatter | solution.py:241
  740.9 3.9 copy-start.42
  744.9 3.8 copy-start.4
  744.9 3.8 copy-start.18
  744.9 3.8 copy-start.28
  744.9 3.8 copy-start.43
  748.7 5.3 copy-start.41
  754.0 3.5 copy-start.1
  754.0 3.5 copy-start.17
  754.0 3.6 copy-start.29
  757.6 3.5 copy-start.36
  761.8 27.7 %reduce-scatter.10.cloned.1.call-start = ((), (), s32[]{:S(2)}) async-start(), calls=%async_computation.16 | async-start | bytes 393216 | tf_op jit(solution)/shard_map/reduce_scatter | solution.py:238
  761.9 4.7 copy-start.2
  761.9 6.7 copy-start.10
  761.9 6.7 copy-start.53
  766.3 3.2 copy-start.7
  770.3 4.6 copy-start.49
  771.8 89.3 %reduce-scatter.18.cloned.1.call-start = ((), (), s32[]{:S(2)}) async-start(), calls=%async_computation.20 | async-start | bytes 1179648 | tf_op jit(solution)/shard_map/reduce_scatter | solution.py:274
  777.4 147.2 %reduce-scatter.16.cloned.1.call-start = ((), (), s32[]{:S(2)}) async-start(), calls=%async_computation.19 | async-start | bytes 1179648 | tf_op jit(solution)/shard_map/reduce_scatter | solution.py:274
  793.0 281.6 %reduce-scatter.20.cloned.1.call-start = ((), (), s32[]{:S(2)}) async-start(), calls=%async_computation.21 | async-start | bytes 9437184 | tf_op jit(solution)/shard_map/reduce_scatter | solution.py:274
  799.3 425.4 %reduce-scatter.14.cloned.1.call-start = ((), (), s32[]{:S(2)}) async-start(), calls=%async_computation.18 | async-start | bytes 9437184 | tf_op jit(solution)/shard_map/reduce_scatter | solution.py:274
  809.1 792.1 %reduce-scatter.26.cloned.1.call-start = ((), (), s32[]{:S(2)}) async-start(), calls=%async_computation.24 | async-start | bytes 25952256 | tf_op jit(solution)/shard_map/reduce_scatter | solution.py:274
  821.8 1155.1 %reduce-scatter.24.cloned.1.call-start = ((), (), s32[]{:S(2)}) async-start(), calls=%async_computation.23 | async-start | bytes 25952256 | tf_op jit(solution)/shard_map/reduce_scatter | solution.py:274
  834.5 1518.1 %reduce-scatter.22.cloned.1.call-start = ((), (), s32[]{:S(2)}) async-start(), calls=%async_computation.22 | async-start | bytes 25952256 | tf_op jit(solution)/shard_map/reduce_scatter | solution.py:274
  847.4 1535.7 %all-reduce.15.cloned.1.call-start = ((), (), s32[]{:S(2)}) async-start(), calls=%async_computation.25 | async-start | bytes 8388608 | tf_op jit(solution)/shard_map/psum | solution.py:73
  847.4 9.4 copy-start.24
  847.4 9.4 copy-start.58
  861.0 1780.8 %all-reduce.17.cloned.1.call-start = ((), (), s32[]{:S(2)}) async-start(), calls=%async_computation.26 | async-start | bytes 22020096 | tf_op jit(solution)/shard_map/psum | solution.py:301
  2352.6 32.8 %copy-start.52 = (f32[2048]{0:T(1024)S(1)}, f32[2048]{0:T(1024)}, u32[]{:S(2)}) copy-start(f32[2048]{0:T(1024)} %get-tuple-element.44) | copy-start | bytes 24580
  2352.6 75.9 %copy-start.56 = (f32[256]{0:T(256)S(1)}, f32[256]{0:T(256)}, u32[]{:S(2)}) copy-start(f32[256]{0:T(256)} %get-tuple-element.82) | copy-start | bytes 3076
  2641.9 3.5 copy-start.34
  2645.3 3.3 copy-start.14
  (32 other events, 51.5 us)
Sparse Core Ops, SparseCore 0:
  10.1 86.2 all-gather.7
  98.6 72.0 all-gather.9
  175.6 19.8 all-reduce.10
  197.5 164.4 all-gather.13
  364.1 161.4 all-gather.11
  527.7 161.4 all-gather.15
  716.3 19.4 all-reduce.12
  761.9 12.9 reduce-scatter.11
  777.7 11.7 reduce-scatter.9
  793.3 64.1 reduce-scatter.17
  861.5 63.0 reduce-scatter.15
  928.1 146.3 reduce-scatter.19
  1078.2 146.5 reduce-scatter.13
  1228.5 372.7 reduce-scatter.25
  1605.0 371.8 reduce-scatter.23
  1980.6 371.8 reduce-scatter.21
  2355.5 27.5 all-reduce.14
  2386.0 255.8 all-reduce.16
where the time goes:
time: 2670 us; the launch traced here: 2660 us
  waiting for transfers between devices  2270 us (85%)
  blocking collectives  160 us (6%)
  matrix products  144 us (5%)
  other arithmetic  35.2 us (1%)
  local copies, waits for them, and re-layouts  30.6 us (1%)
    reduce_scatter x7, waiting for transfers between devices, body(): lax.psum_scatter((jnp.sum(grad_normed_one * scaled_one, axis=0), contract...  1490 us
    psum x1, waiting for transfers between devices, body(): lax.psum((gain_one_grad, query_grad, key_grad, value_grad, output_grad, g...  208 us
    all_gather x1, waiting for transfers between devices, body(): lax.all_gather(up_weight, 'fsdp', axis=0, tiled=True)  162 us
    all_gather x1, waiting for transfers between devices, body(): lax.all_gather(down_weight, 'fsdp', axis=0, tiled=True)  154 us
    all_gather x1, waiting for transfers between devices, body(): lax.all_gather(gate_weight, 'fsdp', axis=0, tiled=True)  154 us
  transfers between devices with their start and end apart: 18, of which 15 were waited for; matrix products, arithmetic and copies ran while one was open for 5% of the time, Pallas kernels for 0%

commit v1 on v0

--- a/solution.py
+++ b/solution.py
@@ -162,12 +162,37 @@
     residual = tokens + attn_branch
     rms_two = lax.rsqrt(jnp.mean(residual * residual, axis=-1, keepdims=True) + EPSILON)
     scaled_two = residual * rms_two
+
+    def bring_paths_all(here_x):
+        mixed_arr, z2, x_now = (
+            jax.lax.axis_size("fsdp"),
+            jax.lax.axis_index("fsdp"),
+            here_x.shape[0],
+        )
+        steps_seen = tuple(((t, (t + 1) % mixed_arr) for t in range(mixed_arr)))
+        vals = tuple(((t, (t - 1) % mixed_arr) for t in range(mixed_arr)))
+        z_new = jnp.zeros((*here_x.shape[:0], mixed_arr * x_now, *here_x.shape[1:]), here_x.dtype)
+        z_new = lax.dynamic_update_slice_in_dim(z_new, here_x, z2 * x_now, axis=0)
+        placed = r1 = here_x
+        z = mixed_arr // 2
+        for kk in range(1, z + 1):
+            placed = jax.lax.ppermute(placed, axis_name="fsdp", perm=steps_seen)
+            z_new = lax.dynamic_update_slice_in_dim(
+                z_new, placed, (z2 - kk) % mixed_arr * x_now, axis=0
+            )
+            if kk < mixed_arr - z:
+                r1 = jax.lax.ppermute(r1, axis_name="fsdp", perm=vals)
+                z_new = lax.dynamic_update_slice_in_dim(
+                    z_new, r1, (z2 + kk) % mixed_arr * x_now, axis=0
+                )
+        return z_new
+
     gate_lin, up_lin, normed_two, gain_two = normed_fold(
         scaled_two,
         (
             lax.all_gather(mlp_gain, "fsdp", axis=0, tiled=True),
             lax.all_gather(gate_weight, "fsdp", axis=0, tiled=True),
-            lax.all_gather(up_weight, "fsdp", axis=0, tiled=True),
+            bring_paths_all(up_weight),
         ),
     )
     silu_value = gate_lin / (1.0 + jnp.exp(-gate_lin))

time: 2670 us -> 2770 us (1.037)
  blocking collectives: 160 us -> 216 us
    ppermute x0 -> x7, waiting for transfers between devices: none -> 199 us  [the longest x4 156 us: bring_paths_all(): placed = jax.lax.ppermute(placed, axis_name='fsdp', perm=steps_seen)]
    all_gather x1, waiting for transfers between devices: 154 us -> 0.01 us  [body(): lax.all_gather(down_weight, 'fsdp', axis=0, tiled=True)]
    all_gather x1, blocking collectives: 18.3 us -> 74.3 us  [body(): lax.all_gather(mlp_gain, 'fsdp', axis=0, tiled=True)]
  transfers between devices with their start and end apart: 18 -> 25, of which waited for: 15 -> 17; matrix products, arithmetic and copies ran while one was open for 5% -> 6% of each run, Pallas kernels for 0% -> 0%
where the time goes in v1:
time: 2770 us; the launch traced here: 2760 us
  waiting for transfers between devices  2280 us (82%)
  blocking collectives  216 us (8%)
  matrix products  135 us (5%)
  local copies, waits for them, and re-layouts  52.3 us (2%)
  other arithmetic  30.8 us (1%)
    reduce_scatter x7, waiting for transfers between devices, body(): lax.psum_scatter((jnp.sum(grad_normed_one * scaled_one, axis=0), contract...  1490 us
    psum x1, waiting for transfers between devices, body(): lax.psum((gain_one_grad, query_grad, key_grad, value_grad, output_grad, g...  208 us
    ppermute x4, waiting for transfers between devices, bring_paths_all(): placed = jax.lax.ppermute(placed, axis_name='fsdp', perm=steps_seen)  156 us
    all_gather x1, waiting for transfers between devices, body(): lax.all_gather(gate_weight, 'fsdp', axis=0, tiled=True)  142 us
    all_gather x1, waiting for transfers between devices, body(): lax.all_gather(up_weight, 'fsdp', axis=0, tiled=True)  140 us
    all_gather x1, blocking collectives, body(): lax.all_gather(mlp_gain, 'fsdp', axis=0, tiled=True)  74.3 us
  transfers between devices with their start and end apart: 25, of which 17 were waited for; matrix products, arithmetic and copies ran while one was open for 6% of the time, Pallas kernels for 0%

profile of v1, /device:TPU:0, one launch (start us, length us, event | category | flops | bytes accessed | tf_op | source)
XLA Modules:
  0.0 2757.2 jit_solution(8583999005342605643)
XLA Ops:
  9.4 22.6 all-gather
  34.4 33.6 %all_gather.42 = bf16[2048,128]{1,0:T(8,128)(2,1)S(1)} all-gather(bf16[256,128]{1,0:T(8,128)(2,1)S(1)} %copy-done.45), channel_id=1, replica_groups=mesh['fsdp'=8,'ctx'=2,'tp'=2] {'fsdp'}, dimensions={0}, use_global_device_ids=true | all-gather | bytes 589824 | tf_op jit(solution)/shard_map/all_gather | solution.py:105
  68.6 5.0 all_gather.43
  73.7 32.5 %all_gather.40 = bf16[2048,128]{1,0:T(8,128)(2,1)S(1)} all-gather(bf16[256,128]{1,0:T(8,128)(2,1)S(1)} %copy-done.46), channel_id=1, replica_groups=mesh['fsdp'=8,'ctx'=2,'tp'=2] {'fsdp'}, dimensions={0}, use_global_device_ids=true | all-gather | bytes 589824 | tf_op jit(solution)/shard_map/all_gather | solution.py:106
  106.7 5.0 all_gather.41
  112.5 3.5 fusion.62
  129.8 41.0 %all-gather.10.cloned.1.call-done = bf16[2048,1024]{1,0:T(8,128)(2,1)} async-done(((bf16[256,1024]{1,0:T(8,128)(2,1)}), bf16[2048,1024]{1,0:T(8,128)(2,1)}) %all-gather.10.cloned.1.call-update) | async-done | bytes 4194320 | tf_op jit(solution)/shard_map/all_gather | solution.py:160
  170.9 4.8 fusion.44
  178.1 4.2 collective-permute-start.1
  182.3 71.8 %collective-permute-done = bf16[256,2816]{1,0:T(8,128)(2,1)S(1)} collective-permute-done((bf16[256,2816]{1,0:T(8,128)(2,1)S(1)}, bf16[256,2816]{1,0:T(8,128)(2,1)S(1)}, u32[]{:S(2)}, u32[]{:S(2)}) %collective-permute-start) | collective-permute-done | bytes 1441824 | tf_op jit(solution)/shard_map/ppermute | solution.py:179
  256.6 3.6 collective-permute-start.3
  260.2 84.5 %collective-permute-done.2 = bf16[256,2816]{1,0:T(8,128)(2,1)} collective-permute-done((bf16[256,2816]{1,0:T(8,128)(2,1)S(1)}, bf16[256,2816]{1,0:T(8,128)(2,1)}, u32[]{:S(2)}, u32[]{:S(2)}) %collective-permute-start.2) | collective-permute-done | bytes 1441824 | tf_op jit(solution)/shard_map/ppermute | solution.py:179
  347.3 74.3 %all-gather.1 = bf16[8,1,256]{2,1,0:T(2,128)(2,1)S(1)} all-gather(bf16[1,1,256]{2,1,0:T(2,128)(2,1)S(1)} %reshape.192), channel_id=1, replica_groups=mesh['fsdp'=8,'ctx'=2,'tp'=2] {'fsdp'}, dimensions={0}, use_global_device_ids=true | all-gather | bytes 4608 | tf_op jit(solution)/shard_map/all_gather | solution.py:193
  421.7 4.9 broadcast_in_dim.28
  434.4 2.6 constant_dynamic-update-slice_fusion.4
  442.1 42.7 %collective-permute-done.5 = bf16[256,2816]{1,0:T(8,128)(2,1)S(1)} collective-permute-done((bf16[256,2816]{1,0:T(8,128)(2,1)}, bf16[256,2816]{1,0:T(8,128)(2,1)S(1)}, u32[]{:S(2)}, u32[]{:S(2)}) %collective-permute-start.5) | collective-permute-done | bytes 1441824 | tf_op jit(solution)/shard_map/ppermute | solution.py:184
  491.9 9.3 fusion.75
  501.2 141.6 %all-gather.12.cloned.1.call-done = bf16[2048,2816]{1,0:T(8,128)(2,1)} async-done(((bf16[256,2816]{1,0:T(8,128)(2,1)}), bf16[2048,2816]{1,0:T(8,128)(2,1)}) %all-gather.12.cloned.1.call-update) | async-done | bytes 11534352 | tf_op jit(solution)/shard_map/all_gather | solution.py:194
  642.8 6.7 fusion.73
  649.5 11.6 multiply_convert_fusion
  662.2 4.5 fusion.76
  666.7 139.6 %all-gather.16.cloned.1.call-done = bf16[2048,2816]{1,0:T(8,128)(2,1)} async-done(((bf16[256,2816]{1,0:T(8,128)(2,1)}), bf16[2048,2816]{1,0:T(8,128)(2,1)}) %all-gather.16.cloned.1.call-update) | async-done | bytes 11534352 | tf_op jit(solution)/shard_map/all_gather | solution.py:216
  806.3 9.8 convolution_add_fusion.2
  816.1 8.5 reduce-scatter.10.cloned.1.call-start
  827.3 8.4 all-reduce.13.cloned.1.call-done
  835.8 2.9 multiply_reduce_fusion
  846.6 3.4 fusion
  857.9 3.1 fusion.34
  863.0 7.9 reduce-scatter.10.cloned.1.call-done
  875.1 10.4 reduce-scatter.12.cloned.1.call-done
  892.2 4.7 fusion.60
  897.2 6.3 fusion.40
  903.6 12.7 fusion.78
  916.4 12.6 fusion.79
  929.1 12.6 convolution_bitcast_fusion
  942.0 9.4 fusion.74
  955.7 65.2 %reduce-scatter.18.cloned.1.call-done = f32[256,128]{1,0:T(8,128)} async-done(((f32[2048,128]{1,0:T(8,128)}), f32[256,128]{1,0:T(8,128)}) %reduce-scatter.18.cloned.1.call-update) | async-done | bytes 131088 | tf_op jit(solution)/shard_map/reduce_scatter | solution.py:299
  1020.9 150.0 %reduce-scatter.14.cloned.1.call-done = f32[256,1024]{1,0:T(8,128)} async-done(((f32[2048,1024]{1,0:T(8,128)}), f32[256,1024]{1,0:T(8,128)}) %reduce-scatter.14.cloned.1.call-update) | async-done | bytes 1048592 | tf_op jit(solution)/shard_map/reduce_scatter | solution.py:299
  1170.9 150.2 %reduce-scatter.20.cloned.1.call-done = f32[256,1024]{1,0:T(8,128)} async-done(((f32[2048,1024]{1,0:T(8,128)}), f32[256,1024]{1,0:T(8,128)}) %reduce-scatter.20.cloned.1.call-update) | async-done | bytes 1048592 | tf_op jit(solution)/shard_map/reduce_scatter | solution.py:299
  1321.1 375.9 %reduce-scatter.22.cloned.1.call-done = f32[256,2816]{1,0:T(8,128)} async-done(((f32[2048,2816]{1,0:T(8,128)}), f32[256,2816]{1,0:T(8,128)}) %reduce-scatter.22.cloned.1.call-update) | async-done | bytes 2883600 | tf_op jit(solution)/shard_map/reduce_scatter | solution.py:299
  1697.0 375.9 %reduce-scatter.24.cloned.1.call-done = f32[256,2816]{1,0:T(8,128)} async-done(((f32[2048,2816]{1,0:T(8,128)}), f32[256,2816]{1,0:T(8,128)}) %reduce-scatter.24.cloned.1.call-update) | async-done | bytes 2883600 | tf_op jit(solution)/shard_map/reduce_scatter | solution.py:299
  2073.0 376.5 %reduce-scatter.26.cloned.1.call-done = f32[256,2816]{0,1:T(8,128)} async-done(((f32[2048,2816]{0,1:T(8,128)}), f32[256,2816]{0,1:T(8,128)}) %reduce-scatter.26.cloned.1.call-update) | async-done | bytes 2883600 | tf_op jit(solution)/shard_map/reduce_scatter | solution.py:299
  2451.3 28.6 %all-reduce.15.cloned.1.call-done = (f32[256,2048]{1,0:T(8,128)}, f32[256,2048]{1,0:T(8,128)}) async-done(((f32[256,2048]{1,0:T(8,128)}, f32[256,2048]{1,0:T(8,128)}), (f32[256,2048]{1,0:T(8,128)}, f32[256,2048]{1,0:T(8,128)})) %all-reduce.15.cloned.1.call-update) | async-done | bytes 4194320 | tf_op jit(solution)/shard_map/psum | solution.py:73
  2482.2 37.3 %all-reduce.2 = (f32[2048]{0:T(1024)S(1)}, f32[2048]{0:T(1024)S(1)}) all-reduce(f32[2048]{0:T(1024)S(1)} %get-tuple-element.46, f32[2048]{0:T(1024)S(1)} %copy-done.51), channel_id=4, replica_groups=mesh['fsdp'=8,'ctx'=2,'tp'=2] {'fsdp'}, use_global_device_ids=true, to_apply=%region_17.18.clone | all-reduce | flops 4096 | bytes 32768
  2519.7 5.7 all-reduce.4
  2525.4 5.1 fusion.21
  2530.5 208.2 %all-reduce.17.cloned.1.call-done = (f32[256,1024]{1,0:T(8,128)}, f32[256,128]{1,0:T(8,128)}, f32[256,128]{1,0:T(8,128)}, f32[256,1024]{1,0:T(8,128)}, f32[256,2...) async-done(((f32[256,1024]{1,0:T(8,128)}, f32[256,128]{1,0:T(8,128)}, f32[256,128]{1,0:T(8,128)}, f32[256,1024]{1,0:T(8,128)}, f32[256,2816]{1,0:T(8,128)}, ...) | async-done | bytes 11010064 | tf_op jit(solution)/shard_map/psum | solution.py:326
  2738.7 3.5 copy.89
  (263 shorter events, 96.0 us)
Async XLA Ops:
  7.2 105.3 %all-gather.8.cloned.1.call-start = ((), (), s32[]{:S(2)}) async-start(), calls=%async_computation.9 | async-start | bytes 4718592 | tf_op jit(solution)/shard_map/all_gather | solution.py:104
  7.9 25.6 copy-start.5
  7.9 162.9 %all-gather.10.cloned.1.call-start = ((), (), s32[]{:S(2)}) async-start(), calls=%async_computation.10 | async-start | bytes 4718592 | tf_op jit(solution)/shard_map/all_gather | solution.py:160
  8.7 478.6 %all-reduce.11.cloned.1.call-start = ((), (), s32[]{:S(2)}) async-start(), calls=%async_computation.11 | async-start | bytes 4194304 | tf_op jit(solution)/shard_map/psum | solution.py:73
  33.8 39.9 %copy-start.46 = (bf16[256,128]{1,0:T(8,128)(2,1)S(1)}, bf16[256,128]{1,0:T(8,128)(2,1)}, u32[]{:S(2)}) copy-start(bf16[256,128]{1,0:T(8,128)(2,1)} %param.17) | copy-start | bytes 196612
  34.4 78.1 %copy-start.47 = (f32[256]{0:T(256)}, f32[256]{0:T(256)S(1)}, u32[]{:S(2)}) copy-start(f32[256]{0:T(256)S(1)} %get-tuple-element.83) | copy-start | bytes 3076
  68.0 38.7 %copy-start.20 = (bf16[2048,128]{1,0:T(8,128)(2,1)}, bf16[2048,128]{1,0:T(8,128)(2,1)S(1)}, u32[]{:S(2)}) copy-start(bf16[2048,128]{1,0:T(8,128)(2,1)S(1)} %all_gather.42) | copy-start | bytes 1572868
  106.2 5.6 copy-start.22
  129.0 41.9 %copy-start.37 = (bf16[64,8,256]{2,0,1:T(8,128)(2,1)}, bf16[64,8,256]{2,0,1:T(8,128)(2,1)S(1)}, u32[]{:S(2)}) copy-start(bf16[64,8,256]{2,0,1:T(8,128)(2,1)S(1)} %fusion.29) | copy-start | bytes 786436
  129.8 45.9 %copy-start.38 = (bf16[64,8,256]{2,0,1:T(8,128)(2,1)}, bf16[64,8,256]{2,0,1:T(8,128)(2,1)S(1)}, u32[]{:S(2)}) copy-start(bf16[64,8,256]{2,0,1:T(8,128)(2,1)S(1)} %fusion.30) | copy-start | bytes 786436
  175.7 171.6 %copy-start.58 = (bf16[256]{0:T(256)(128)(2,1)S(1)}, bf16[256]{0:T(256)(128)(2,1)}, u32[]{:S(2)}) copy-start(bf16[256]{0:T(256)(128)(2,1)} %param.19) | copy-start | bytes 1540
  175.7 316.1 %all-gather.14.cloned.1.call-start = ((), (), s32[]{:S(2)}) async-start(), calls=%async_computation.13 | async-start | bytes 12976128 | tf_op jit(solution)/shard_map/all_gather | solution.py:201
  176.3 466.5 %all-gather.12.cloned.1.call-start = ((), (), s32[]{:S(2)}) async-start(), calls=%async_computation.12 | async-start | bytes 12976128 | tf_op jit(solution)/shard_map/all_gather | solution.py:194
  176.9 629.5 %all-gather.16.cloned.1.call-start = ((), (), s32[]{:S(2)}) async-start(), calls=%async_computation.14 | async-start | bytes 12976128 | tf_op jit(solution)/shard_map/all_gather | solution.py:216
  177.5 658.3 %all-reduce.13.cloned.1.call-start = ((), (), s32[]{:S(2)}) async-start(), calls=%async_computation.15 | async-start | bytes 4194304 | tf_op jit(solution)/shard_map/psum | solution.py:73
  177.5 76.6 %collective-permute-start = (bf16[256,2816]{1,0:T(8,128)(2,1)S(1)}, bf16[256,2816]{1,0:T(8,128)(2,1)S(1)}, u32[]{:S(2)}, u32[]{:S(2)}) collective-permute-start(bf16[256,2816]{1,0:T(8,128)(2,1)S(1)} %copy-done.12), channel_id=1, source_target_pairs={{0,4},{4,8},{8,12},{12,16},{16,20},{20,24},{24,28},{28,0},{1,5},{5... | collective-permute-start | bytes 4325384 | tf_op jit(solution)/shard_map/ppermute | solution.py:179
  178.1 78.5 %collective-permute-start.1 = (bf16[256,2816]{1,0:T(8,128)(2,1)S(1)}, bf16[256,2816]{1,0:T(8,128)(2,1)}, u32[]{:S(2)}, u32[]{:S(2)}) collective-permute-start(bf16[256,2816]{1,0:T(8,128)(2,1)S(1)} %copy-done.12), channel_id=1, source_target_pairs={{0,28},{4,0},{8,4},{12,8},{16,12},{20,16},{24,20},{28,24},{1,29},{... | collective-permute-start | bytes 4325384 | tf_op jit(solution)/shard_map/ppermute | solution.py:184
  254.1 90.6 %collective-permute-start.2 = (bf16[256,2816]{1,0:T(8,128)(2,1)S(1)}, bf16[256,2816]{1,0:T(8,128)(2,1)}, u32[]{:S(2)}, u32[]{:S(2)}) collective-permute-start(bf16[256,2816]{1,0:T(8,128)(2,1)S(1)} %collective-permute-done), channel_id=1, source_target_pairs={{0,4},{4,8},{8,12},{12,16},{16,20},{20,24},{24,28},{28,0},{1,5},{5... | collective-permute-start | bytes 4325384 | tf_op jit(solution)/shard_map/ppermute | solution.py:179
  256.6 173.2 %collective-permute-start.3 = (bf16[256,2816]{1,0:T(8,128)(2,1)}, bf16[256,2816]{1,0:T(8,128)(2,1)}, u32[]{:S(2)}, u32[]{:S(2)}) collective-permute-start(bf16[256,2816]{1,0:T(8,128)(2,1)} %collective-permute-done.1), channel_id=1, source_target_pairs={{0,28},{4,0},{8,4},{12,8},{16,12},{20,16},{24,20},{28,24},{1,29},{... | collective-permute-start | bytes 4325384 | tf_op jit(solution)/shard_map/ppermute | solution.py:184
  344.7 87.6 %collective-permute-start.4 = (bf16[256,2816]{1,0:T(8,128)(2,1)}, bf16[256,2816]{1,0:T(8,128)(2,1)}, u32[]{:S(2)}, u32[]{:S(2)}) collective-permute-start(bf16[256,2816]{1,0:T(8,128)(2,1)} %collective-permute-done.2), channel_id=1, source_target_pairs={{0,4},{4,8},{8,12},{12,16},{16,20},{20,24},{24,28},{28,0},{1,5},{5... | collective-permute-start | bytes 4325384 | tf_op jit(solution)/shard_map/ppermute | solution.py:179
  429.7 55.0 %collective-permute-start.5 = (bf16[256,2816]{1,0:T(8,128)(2,1)}, bf16[256,2816]{1,0:T(8,128)(2,1)S(1)}, u32[]{:S(2)}, u32[]{:S(2)}) collective-permute-start(bf16[256,2816]{1,0:T(8,128)(2,1)} %collective-permute-done.3), channel_id=1, source_target_pairs={{0,28},{4,0},{8,4},{12,8},{16,12},{20,16},{24,20},{28,24},{1,29},{... | collective-permute-start | bytes 4325384 | tf_op jit(solution)/shard_map/ppermute | solution.py:184
  432.3 53.7 %collective-permute-start.6 = (bf16[256,2816]{1,0:T(8,128)(2,1)}, bf16[256,2816]{1,0:T(8,128)(2,1)S(1)}, u32[]{:S(2)}, u32[]{:S(2)}) collective-permute-start(bf16[256,2816]{1,0:T(8,128)(2,1)} %collective-permute-done.4), channel_id=1, source_target_pairs={{0,4},{4,8},{8,12},{12,16},{16,20},{20,24},{24,28},{28,0},{1,5},{5... | collective-permute-start | bytes 4325384 | tf_op jit(solution)/shard_map/ppermute | solution.py:179
  642.8 6.7 copy-start.10
  642.8 6.7 copy-start.60
  642.8 19.5 slice-start
  642.8 19.5 slice-start.1
  649.5 12.7 slice-start.2
  816.1 54.8 %reduce-scatter.10.cloned.1.call-start = ((), (), s32[]{:S(2)}) async-start(), calls=%async_computation.16 | async-start | bytes 393216 | tf_op jit(solution)/shard_map/reduce_scatter | solution.py:263
  842.2 4.4 copy-start.42
  846.6 3.6 copy-start.1
  857.8 27.7 %reduce-scatter.12.cloned.1.call-start = ((), (), s32[]{:S(2)}) async-start(), calls=%async_computation.17 | async-start | bytes 393216 | tf_op jit(solution)/shard_map/reduce_scatter | solution.py:266
  857.9 3.6 copy-start.4
  863.0 92.7 %reduce-scatter.16.cloned.1.call-start = ((), (), s32[]{:S(2)}) async-start(), calls=%async_computation.19 | async-start | bytes 1179648 | tf_op jit(solution)/shard_map/reduce_scatter | solution.py:299
  871.8 13.7 copy-start.48
  875.0 13.0 copy-start.32
  875.1 145.9 %reduce-scatter.18.cloned.1.call-start = ((), (), s32[]{:S(2)}) async-start(), calls=%async_computation.20 | async-start | bytes 1179648 | tf_op jit(solution)/shard_map/reduce_scatter | solution.py:299
  888.0 282.9 %reduce-scatter.14.cloned.1.call-start = ((), (), s32[]{:S(2)}) async-start(), calls=%async_computation.18 | async-start | bytes 9437184 | tf_op jit(solution)/shard_map/reduce_scatter | solution.py:299
  896.9 424.2 %reduce-scatter.20.cloned.1.call-start = ((), (), s32[]{:S(2)}) async-start(), calls=%async_computation.21 | async-start | bytes 9437184 | tf_op jit(solution)/shard_map/reduce_scatter | solution.py:299
  903.6 793.5 %reduce-scatter.22.cloned.1.call-start = ((), (), s32[]{:S(2)}) async-start(), calls=%async_computation.22 | async-start | bytes 25952256 | tf_op jit(solution)/shard_map/reduce_scatter | solution.py:299
  916.4 1156.6 %reduce-scatter.24.cloned.1.call-start = ((), (), s32[]{:S(2)}) async-start(), calls=%async_computation.23 | async-start | bytes 25952256 | tf_op jit(solution)/shard_map/reduce_scatter | solution.py:299
  929.0 1520.4 %reduce-scatter.26.cloned.1.call-start = ((), (), s32[]{:S(2)}) async-start(), calls=%async_computation.24 | async-start | bytes 25952256 | tf_op jit(solution)/shard_map/reduce_scatter | solution.py:299
  941.7 1538.2 %all-reduce.15.cloned.1.call-start = ((), (), s32[]{:S(2)}) async-start(), calls=%async_computation.25 | async-start | bytes 8388608 | tf_op jit(solution)/shard_map/psum | solution.py:73
  942.0 9.4 copy-start.25
  942.0 9.4 copy-start.56
  955.6 1783.1 %all-reduce.17.cloned.1.call-start = ((), (), s32[]{:S(2)}) async-start(), calls=%async_computation.26 | async-start | bytes 22020096 | tf_op jit(solution)/shard_map/psum | solution.py:326
  2449.5 32.7 %copy-start.51 = (f32[2048]{0:T(1024)S(1)}, f32[2048]{0:T(1024)}, u32[]{:S(2)}) copy-start(f32[2048]{0:T(1024)} %get-tuple-element.44) | copy-start | bytes 24580
  2449.5 75.9 %copy-start.54 = (f32[256]{0:T(256)S(1)}, f32[256]{0:T(256)}, u32[]{:S(2)}) copy-start(f32[256]{0:T(256)} %get-tuple-element.82) | copy-start | bytes 3076
  2738.7 3.5 copy-start.35
  (41 other events, 75.5 us)
Sparse Core Ops, SparseCore 0:
  10.1 86.6 all-gather.7
  98.9 71.9 all-gather.9
  175.8 19.8 all-reduce.10
  197.7 265.4 all-gather.13
  465.2 177.4 all-gather.11
  644.8 161.4 all-gather.15
  816.3 19.4 all-reduce.12
  857.9 12.9 reduce-scatter.9
  873.7 11.7 reduce-scatter.11
  889.3 64.2 reduce-scatter.15
  957.6 63.2 reduce-scatter.17
  1024.4 146.4 reduce-scatter.13
  1174.5 146.5 reduce-scatter.19
  1324.9 372.1 reduce-scatter.21
  1700.8 372.1 reduce-scatter.23
  2076.7 372.6 reduce-scatter.25
  2452.4 27.4 all-reduce.14
  2482.8 255.8 all-reduce.16
